TPU v7x, 32 devices: a whole 2x2x4 slice. The times are simulated.
32 devices in a mesh: groups: 2 (over y), seq: 4 (over z), head: 2 (over x), sub: 2 (over core).
Axes of the slice: x: 2, y: 2, z: 4, core: 2. Of those that a mesh axis runs over, the one named last changes fastest.
Arguments:
- queries: bfloat16 [4608, 8192], P(('groups', 'seq'), ('head', 'sub')), parts along dimension 0, may hold values from -6 to 6
- keys: bfloat16 [4608, 8192], P(('groups', 'seq'), ('head', 'sub')), parts along dimension 0, may hold values from -0.0546875 to 0.0546875
- values: bfloat16 [4608, 8192], P(('groups', 'seq'), ('head', 'sub')), parts along dimension 0, may hold values from -800 to 800
- decay_exp: int32 [64], P(('head', 'sub')), may hold values from 1 to 2303, as said below
- gain: float32 [8192], P(('head', 'sub')), may hold values from 0.5 to 1.5
Outputs:
- normed: bfloat16 [4608, 8192], P(('groups', 'seq'), ('head', 'sub')), parts along dimension 0
- final_state: float32 [128, 128, 128], P(('groups', 'head', 'sub'), 'seq'), parts along dimension 0
There are 2 independent parts, one for each index of `groups`. A program takes and returns all parts, laid end to end along the dimension named above; an argument that names none is the same for every part. Nothing has to cross between parts.
Inputs may be any that keep to these rules, and one draw needn't show every extreme that they name: The decay of head h over one position is 2 ** (-decay_exp[h] / 18432).
All inputs are finite; a program needn't handle non-finite values.
Results may differ from a plain program's by a relative error of at most 0.0049.
Values sent between devices are 32-bit elements; how exact they have to be, the bound alone decides.
A program may use at most 64 MiB of HBM per device.

v0:
```python
import jax
import jax.numpy as jnp
from jax import lax
from jax.sharding import PartitionSpec as P

HEADS = 64
DK = 128


def local(queries, keys, values, decay_exp, gain):
    tokens = queries.shape[0]
    heads_here = decay_exp.shape[0]
    head_size = queries.shape[1] // heads_here
    n_seq = lax.axis_size("seq")
    decay_rate = decay_exp.astype(jnp.float32) / (8.0 * tokens * n_seq)
    offsets = jnp.arange(tokens).astype(jnp.float32)
    distance = offsets[:, None] - offsets[None, :]
    causal = distance >= 0
    within = jnp.where(
        causal[None], jnp.exp2(-decay_rate[:, None, None] * jnp.maximum(distance, 0.0)[None]), 0.0
    )
    key_decay = jnp.exp2(-decay_rate[None, :] * (tokens - 1.0 - offsets)[:, None])
    query_decay = jnp.exp2(-decay_rate[None, :] * (offsets + 1.0)[:, None])
    query_heads = queries.reshape(tokens, heads_here, head_size)
    key_heads = keys.reshape(tokens, heads_here, head_size)
    value_heads = values.reshape(tokens, heads_here, head_size)
    scaled_keys = (key_heads.astype(jnp.float32) * key_decay[:, :, None]).astype(jnp.bfloat16)
    local_state = jnp.einsum(
        "ihd,ihe->hde", scaled_keys, value_heads, preferred_element_type=jnp.float32
    )
    row_pieces = lax.all_to_all(local_state[None], "seq", split_axis=2, concat_axis=0, tiled=True)
    ranks = jnp.arange(n_seq).astype(jnp.float32)
    gap = ranks[:, None] - 1.0 - ranks[None, :]
    prior = jnp.where(
        gap[:, :, None] >= 0,
        jnp.exp2(-decay_rate[None, None, :] * tokens * jnp.maximum(gap, 0.0)[:, :, None]),
        0.0,
    )
    toward_end = jnp.exp2(-decay_rate[None, :] * tokens * (n_seq - 1.0 - ranks)[:, None])
    prefix_by_block = jnp.einsum(
        "bmh,mhre->bhre", prior, row_pieces, precision=lax.Precision.HIGHEST
    )
    final_rows = jnp.einsum("mh,mhre->hre", toward_end, row_pieces, precision=lax.Precision.HIGHEST)
    prefix = lax.all_to_all(prefix_by_block, "seq", split_axis=0, concat_axis=2, tiled=True)[0]
    scores = jnp.einsum("ihd,jhd->hij", query_heads, key_heads, preferred_element_type=jnp.float32)
    weights = (scores * within).astype(jnp.bfloat16)
    intra = jnp.einsum("hij,jhd->ihd", weights, value_heads, preferred_element_type=jnp.float32)
    decayed_query = query_heads.astype(jnp.float32) * query_decay[:, :, None]
    inter = jnp.einsum("ihd,hde->ihe", decayed_query, prefix, precision=lax.Precision.HIGHEST)
    mixed = (intra + inter).reshape(tokens, heads_here * head_size)
    squares = jnp.sum(mixed * mixed, axis=1)
    summed = lax.psum(squares, ("head", "sub"))
    mean_square = summed / (HEADS * DK)
    normed = (mixed * lax.rsqrt(mean_square + 1e-06)[:, None] * gain[None, :]).astype(jnp.bfloat16)
    return (normed, final_rows)


def solution(mesh):
    return jax.shard_map(
        local,
        mesh=mesh,
        in_specs=(
            P(("groups", "seq"), ("head", "sub")),
            P(("groups", "seq"), ("head", "sub")),
            P(("groups", "seq"), ("head", "sub")),
            P(("head", "sub")),
            P(("head", "sub")),
        ),
        out_specs=(
            P(("groups", "seq"), ("head", "sub")),
            P(("groups", "head", "sub"), "seq", None),
        ),
        check_vma=False,
    )
```

profile of v0, /device:TPU:0, one launch (start us, length us, event | category | flops | bytes accessed | tf_op | source)
XLA Modules:
  0.0 92.8 jit_solution(15200276459177829985)
XLA Ops:
  0.6 0.0 copy-start
  0.7 0.8 broadcast_multiply_fusion
  1.5 0.1 multiply_exponential_fusion
  1.6 4.7 %fusion.30 = f32[1,16,128,128]{3,2,1,0:T(8,128)S(1)} fusion(f32[576,16]{0,1:T(8,128)S(1)} %get-tuple-element.3, bf16[576,2048]{1,0:T(8,128)(2,1)} %param.7, bf16[576,2048]{1,0:T(8,128)(2,1)} %param.6), kind=kOutput, calls=%fused_computation.30 | convolution fusion | flops 305528832 | bytes 5804032 | tf_op jit(solution)/shard_map/ihd,ihe->hde/dot_general | solution.py:28
  6.3 1.6 %copy.34 = f32[1,16,128,128]{3,1,0,2:T(8,128)} copy(f32[1,16,128,128]{3,2,1,0:T(8,128)S(1)} %fusion.30) | data formatting | bytes 2097152 | tf_op jit(solution)/shard_map/broadcast_in_dim | solution.py:31
  7.8 6.3 %all-to-all-start = ((f32[1,16,128,128]{3,1,0,2:T(8,128)}), f32[1,16,128,128]{3,1,0,2:T(8,128)S(1)}, u32[]{:S(2)}, u32[]{:S(2)}) async-start(f32[1,16,128,128]{3,1,0,2:T(8,128)} %copy.34), calls=%async_computation | async-start | bytes 2097152 | tf_op jit(solution)/shard_map/all_to_all | solution.py:31
  14.2 0.1 exponential_bitcast_fusion
  14.3 0.1 copy.42
  14.4 0.1 subtract_compare_fusion.1
  14.4 0.1 subtract_maximum_fusion.1
  14.5 1.1 %subtract_compare_fusion = pred[576,576]{1,0:T(8,128)(4,1)} fusion(f32[576]{0:T(1024)S(1)} %iota_convert_fusion), kind=kLoop, calls=%fused_computation.23 | loop fusion | flops 663552 | bytes 334080 | tf_op jit(solution)/shard_map/ge | solution.py:18
  15.6 1.3 %subtract_maximum_fusion = f32[576,576]{1,0:T(8,128)} fusion(f32[576]{0:T(1024)S(1)} %iota_convert_fusion), kind=kLoop, calls=%fused_computation.22 | loop fusion | flops 663552 | bytes 1329408 | tf_op jit(solution)/shard_map/max | solution.py:20
  16.9 23.1 %all-to-all-done = f32[1,16,128,128]{3,1,0,2:T(8,128)S(1)} async-done(((f32[1,16,128,128]{3,1,0,2:T(8,128)}), f32[1,16,128,128]{3,1,0,2:T(8,128)S(1)}, u32[]{:S(2)}, u32[]{:S(2)}) %all-to-all-start) | async-done | bytes 1048608 | tf_op jit(solution)/shard_map/all_to_all | solution.py:31
  39.9 2.5 %convolution_bitcast_fusion = f32[4,16,32,128]{3,0,2,1:T(4,128)S(1)} fusion(f32[1,16,4,32,128]{4,1,3,2,0:T(8,128)S(1)} %bitcast.93, f32[4,4]{1,0:T(4,128)S(1)} %subtract_maximum_fusion.1, f32[16]{0:T(128)S(1)} %get-tuple-element.4, pred[4,4]{1,0:T(4,128)(4,1)S(1)} %subtract_compare_fusion.1), kind=kOutput, calls=%fused_computation.31 | convolution fusion | flops 12583680 | bytes 2097296 | tf_op jit(solution)/shard_map/bmh,mhre->bhre/dot_general | solution.py:40
  42.4 1.1 %copy.37 = f32[4,16,32,128]{3,2,1,0:T(8,128)} copy(f32[4,16,32,128]{3,0,2,1:T(4,128)S(1)} %convolution_bitcast_fusion) | data formatting | bytes 2097152 | tf_op jit(solution)/shard_map/bmh,mhre->bhre/transpose | solution.py:40
  43.6 4.4 %all-to-all-start.1 = ((f32[4,16,32,128]{3,2,1,0:T(8,128)}), f32[4,16,32,128]{3,2,1,0:T(8,128)}, u32[]{:S(2)}, u32[]{:S(2)}) async-start(f32[4,16,32,128]{3,2,1,0:T(8,128)} %copy.37), calls=%async_computation.1 | async-start | bytes 2097152 | tf_op jit(solution)/shard_map/all_to_all | solution.py:44
  48.0 0.0 copy-done
  48.1 12.4 %fusion = f32[16,576,128]{2,1,0:T(8,128)} fusion(f32[576,576]{1,0:T(8,128)} %subtract_maximum_fusion, f32[16]{0:T(128)S(1)} %get-tuple-element.5, pred[576,576]{1,0:T(8,128)(4,1)} %subtract_compare_fusion, bf16[576,2048]{1,0:T(8,128)(2,1)} %param.7, bf16[576,2048]{1,0:T(8,128)(2,1)} %param.6, bf16[576,2048]{1,0:T(8,128)(2,1)S(1)} %copy-done), kind=kOutput, calls=%fused_computation.1 | convolution fusion | flops 2744451072 | bytes 13455424 | tf_op jit(solution)/shard_map/hij,jhd->ihd/dot_general | solution.py:47
  60.5 3.1 %fusion.33 = f32[16,1,32,128]{3,1,2,0:T(1,128)} fusion(f32[4,16,1,1]{0,2,3,1:T(1,128)S(1)} %copy.42, f32[1,16,4,32,128]{4,1,3,2,0:T(8,128)S(1)} %bitcast.94), kind=kOutput, calls=%fused_computation.32 | convolution fusion | flops 3145728 | bytes 1310976 | tf_op jit(solution)/shard_map/mh,mhre->hre/dot_general | solution.py:43
  63.6 9.6 %all-to-all-done.1 = f32[4,16,32,128]{3,2,1,0:T(8,128)} async-done(((f32[4,16,32,128]{3,2,1,0:T(8,128)}), f32[4,16,32,128]{3,2,1,0:T(8,128)}, u32[]{:S(2)}, u32[]{:S(2)}) %all-to-all-start.1) | async-done | bytes 1048608 | tf_op jit(solution)/shard_map/all_to_all | solution.py:44
  73.2 1.3 %copy.38 = f32[4,16,32,128]{3,2,0,1:T(8,128)S(1)} copy(f32[4,16,32,128]{3,2,1,0:T(8,128)} %all-to-all-done.1) | data formatting | bytes 2097152 | tf_op jit(solution)/shard_map/all_to_all | solution.py:44
  74.5 0.0 copy-start.1
  74.5 8.2 %multiply_reduce_fusion = (f32[576]{0:T(1024)S(1)}, f32[576,16,128]{2,0,1:T(8,128)}) fusion(f32[16,128,128]{2,1,0:T(8,128)S(1)} %bitcast.95, f32[576,16]{0,1:T(8,128)S(1)} %get-tuple-element.2, f32[16,576,128]{2,1,0:T(8,128)} %fusion, bf16[576,2048]{1,0:T(8,128)(2,1)S(1)} %copy-done), kind=kOutput, calls=%fused_computation.8 | convolution fusion | flops 1817837056 | bytes 12884224 | tf_op jit(solution)/shard_map/ihd,hde->ihe/dot_general | solution.py:49
  82.7 5.8 %psum.7 = f32[576]{0:T(1024)S(1)} all-reduce(f32[576]{0:T(1024)S(1)} %get-tuple-element.6), channel_id=1, replica_groups=mesh['groups'=2,'seq'=4,'head'=2,'sub'=2] {'head','sub'}, use_global_device_ids=true, to_apply=%region_1.2 | all-reduce | flops 576 | bytes 4608 | tf_op jit(solution)/shard_map/psum | solution.py:52
  88.6 0.0 copy-done.1
  88.6 4.2 %fusion.5 = bf16[576,2048]{1,0:T(8,128)(2,1)} fusion(f32[2048]{0:T(1024)S(1)} %copy-done.1, f32[576]{0:T(1024)S(1)} %add_rsqrt_fusion, f32[576,16,128]{2,0,1:T(8,128)} %get-tuple-element.7), kind=kLoop, calls=%fused_computation.6 | loop fusion | flops 3538944 | bytes 7088384 | tf_op jit(solution)/shard_map/convert_element_type | solution.py:54
  (6 shorter events, 0.0 us)
Async XLA Ops:
  0.6 47.4 %copy-start = (bf16[576,2048]{1,0:T(8,128)(2,1)S(1)}, bf16[576,2048]{1,0:T(8,128)(2,1)}, u32[]{:S(2)}) copy-start(bf16[576,2048]{1,0:T(8,128)(2,1)} %param.5) | copy-start | bytes 7077892
  7.8 32.1 %all-to-all-start = ((f32[1,16,128,128]{3,1,0,2:T(8,128)}), f32[1,16,128,128]{3,1,0,2:T(8,128)S(1)}, u32[]{:S(2)}, u32[]{:S(2)}) async-start(f32[1,16,128,128]{3,1,0,2:T(8,128)} %copy.34), calls=%async_computation | async-start | bytes 2097152 | tf_op jit(solution)/shard_map/all_to_all | solution.py:31
  43.6 29.6 %all-to-all-start.1 = ((f32[4,16,32,128]{3,2,1,0:T(8,128)}), f32[4,16,32,128]{3,2,1,0:T(8,128)}, u32[]{:S(2)}, u32[]{:S(2)}) async-start(f32[4,16,32,128]{3,2,1,0:T(8,128)} %copy.37), calls=%async_computation.1 | async-start | bytes 2097152 | tf_op jit(solution)/shard_map/all_to_all | solution.py:44
  74.5 14.1 %copy-start.1 = (f32[2048]{0:T(1024)S(1)}, f32[2048]{0:T(1024)}, u32[]{:S(2)}) copy-start(f32[2048]{0:T(1024)} %param.9) | copy-start | bytes 24580
where the time goes:
time: 93.2 us; the launch traced here: 92.8 us
  waiting for transfers between devices  32.7 us (35%)
  matrix products  31 us (33%)
  starting transfers between devices  10.8 us (12%)
  other arithmetic  7.7 us (8%)
  blocking collectives  5.83 us (6%)
  local copies, waits for them, and re-layouts  4.14 us (4%)
    all_to_all x1, waiting for transfers between devices, local(): lax.all_to_all(local_state[None], 'seq', split_axis=2, concat_axis=0, til...  23.1 us
    dot_general x1, matrix products, local(): jnp.einsum('hij,jhd->ihd', weights, value_heads, preferred_element_type=j...  12.4 us
    all_to_all x1, waiting for transfers between devices, local(): lax.all_to_all(prefix_by_block, 'seq', split_axis=0, concat_axis=2, tiled...  9.61 us
    dot_general x1, matrix products, local(): jnp.einsum('ihd,hde->ihe', decayed_query, prefix, precision=lax.Precision...  8.2 us
    all_to_all x1, starting transfers between devices, local(): lax.all_to_all(local_state[None], 'seq', split_axis=2, concat_axis=0, til...  6.35 us
    psum x1, blocking collectives, local(): summed = lax.psum(squares, ('head', 'sub'))  5.83 us
    dot_general x1, matrix products, local(): jnp.einsum('ihd,ihe->hde', scaled_keys, value_heads, preferred_element_ty...  4.7 us
    all_to_all x1, starting transfers between devices, local(): lax.all_to_all(prefix_by_block, 'seq', split_axis=0, concat_axis=2, tiled...  4.44 us
  transfers between devices with their start and end apart: 2, of which 2 were waited for; matrix products, arithmetic and copies ran while one was open for 20% of the time, Pallas kernels for 0%

commit v1 on v0

--- a/solution.py
+++ b/solution.py
@@ -49,7 +49,7 @@
     inter = jnp.einsum("ihd,hde->ihe", decayed_query, prefix, precision=lax.Precision.HIGHEST)
     mixed = (intra + inter).reshape(tokens, heads_here * head_size)
     squares = jnp.sum(mixed * mixed, axis=1)
-    summed = lax.psum(squares, ("head", "sub"))
+    summed = jnp.sum(lax.all_gather(squares, ("head", "sub")), axis=0)
     mean_square = summed / (HEADS * DK)
     normed = (mixed * lax.rsqrt(mean_square + 1e-06)[:, None] * gain[None, :]).astype(jnp.bfloat16)
     return (normed, final_rows)

time: 93.2 us -> 97.8 us (1.049)
  blocking collectives: 5.83 us -> 10.1 us
  waiting for transfers between devices: 32.7 us -> 31.4 us
    unnamed x0 -> x1, blocking collectives: none -> 10.1 us
    psum x1 -> x0, blocking collectives: 5.83 us -> none  [local(): summed = lax.psum(squares, ('head', 'sub'))]
    all_to_all x1, waiting for transfers between devices: 23.1 us -> 21.8 us  [local(): lax.all_to_all(local_state[None], 'seq', split_axis=2, concat_axis=0, til...]
  transfers between devices with their start and end apart: 2 -> 2, of which waited for: 2 -> 2; matrix products, arithmetic and copies ran while one was open for 20% -> 19% of each run, Pallas kernels for 0% -> 0%
where the time goes in v1:
time: 97.8 us; the launch traced here: 97.4 us
  waiting for transfers between devices  31.4 us (32%)
  matrix products  31 us (32%)
  starting transfers between devices  10.8 us (11%)
  blocking collectives  10.1 us (10%)
  other arithmetic  7.72 us (8%)
  local copies, waits for them, and re-layouts  4.98 us (5%)
  between operations  1.4 us (1%)
    all_to_all x1, waiting for transfers between devices, local(): lax.all_to_all(local_state[None], 'seq', split_axis=2, concat_axis=0, til...  21.8 us
    dot_general x1, matrix products, local(): jnp.einsum('hij,jhd->ihd', weights, value_heads, preferred_element_type=j...  12.4 us
    unnamed x1, blocking collectives  10.1 us
    all_to_all x1, waiting for transfers between devices, local(): lax.all_to_all(prefix_by_block, 'seq', split_axis=0, concat_axis=2, tiled...  9.6 us
    dot_general x1, matrix products, local(): jnp.einsum('ihd,hde->ihe', decayed_query, prefix, precision=lax.Precision...  8.21 us
    all_to_all x1, starting transfers between devices, local(): lax.all_to_all(local_state[None], 'seq', split_axis=2, concat_axis=0, til...  6.35 us
    dot_general x1, matrix products, local(): jnp.einsum('ihd,ihe->hde', scaled_keys, value_heads, preferred_element_ty...  4.7 us
    all_to_all x1, starting transfers between devices, local(): lax.all_to_all(prefix_by_block, 'seq', split_axis=0, concat_axis=2, tiled...  4.42 us
  transfers between devices with their start and end apart: 2, of which 2 were waited for; matrix products, arithmetic and copies ran while one was open for 19% of the time, Pallas kernels for 0%

profile of v1, /device:TPU:0, one launch (start us, length us, event | category | flops | bytes accessed | tf_op | source)
XLA Modules:
  0.0 97.4 jit_solution(1171183307595716769)
XLA Ops:
  0.6 0.0 copy-start
  0.7 0.8 broadcast_multiply_fusion
  1.5 0.1 multiply_exponential_fusion
  1.6 4.7 %fusion.30 = f32[1,16,128,128]{3,2,1,0:T(8,128)S(1)} fusion(f32[576,16]{0,1:T(8,128)S(1)} %get-tuple-element.3, bf16[576,2048]{1,0:T(8,128)(2,1)} %param.7, bf16[576,2048]{1,0:T(8,128)(2,1)} %param.6), kind=kOutput, calls=%fused_computation.30 | convolution fusion | flops 305528832 | bytes 5804032 | tf_op jit(solution)/shard_map/ihd,ihe->hde/dot_general | solution.py:28
  6.3 0.0 copy-start.2
  6.3 1.6 %copy.46 = f32[1,16,128,128]{3,1,0,2:T(8,128)} copy(f32[1,16,128,128]{3,2,1,0:T(8,128)S(1)} %fusion.30) | data formatting | bytes 2097152 | tf_op jit(solution)/shard_map/broadcast_in_dim | solution.py:31
  7.9 6.3 %all-to-all-start = ((f32[1,16,128,128]{3,1,0,2:T(8,128)}), f32[1,16,128,128]{3,1,0,2:T(8,128)S(1)}, u32[]{:S(2)}, u32[]{:S(2)}) async-start(f32[1,16,128,128]{3,1,0,2:T(8,128)} %copy.46), calls=%async_computation | async-start | bytes 2097152 | tf_op jit(solution)/shard_map/all_to_all | solution.py:31
  14.2 0.1 exponential_bitcast_fusion
  14.3 0.1 copy.54
  14.4 0.0 copy-done.2
  14.4 0.6 dynamic-slice
  15.7 0.1 subtract_compare_fusion.1
  15.7 0.1 subtract_maximum_fusion.1
  15.8 1.1 %subtract_compare_fusion = pred[576,576]{1,0:T(8,128)(4,1)} fusion(f32[576]{0:T(1024)S(1)} %iota_convert_fusion), kind=kLoop, calls=%fused_computation.23 | loop fusion | flops 663552 | bytes 334080 | tf_op jit(solution)/shard_map/ge | solution.py:18
  16.9 1.3 %subtract_maximum_fusion = f32[576,576]{1,0:T(8,128)} fusion(f32[576]{0:T(1024)S(1)} %iota_convert_fusion), kind=kLoop, calls=%fused_computation.22 | loop fusion | flops 663552 | bytes 1329408 | tf_op jit(solution)/shard_map/max | solution.py:20
  18.1 21.8 %all-to-all-done = f32[1,16,128,128]{3,1,0,2:T(8,128)S(1)} async-done(((f32[1,16,128,128]{3,1,0,2:T(8,128)}), f32[1,16,128,128]{3,1,0,2:T(8,128)S(1)}, u32[]{:S(2)}, u32[]{:S(2)}) %all-to-all-start) | async-done | bytes 1048608 | tf_op jit(solution)/shard_map/all_to_all | solution.py:31
  39.9 2.5 %convolution_bitcast_fusion = f32[4,16,32,128]{3,0,2,1:T(4,128)S(1)} fusion(f32[1,16,4,32,128]{4,1,3,2,0:T(8,128)S(1)} %bitcast.94, f32[4,4]{1,0:T(4,128)S(1)} %subtract_maximum_fusion.1, f32[16]{0:T(128)S(1)} %get-tuple-element.4, pred[4,4]{1,0:T(4,128)(4,1)S(1)} %subtract_compare_fusion.1), kind=kOutput, calls=%fused_computation.31 | convolution fusion | flops 12583680 | bytes 2097296 | tf_op jit(solution)/shard_map/bmh,mhre->bhre/dot_general | solution.py:40
  42.5 1.1 %copy.49 = f32[4,16,32,128]{3,2,1,0:T(8,128)} copy(f32[4,16,32,128]{3,0,2,1:T(4,128)S(1)} %convolution_bitcast_fusion) | data formatting | bytes 2097152 | tf_op jit(solution)/shard_map/bmh,mhre->bhre/transpose | solution.py:40
  43.6 4.4 %all-to-all-start.1 = ((f32[4,16,32,128]{3,2,1,0:T(8,128)}), f32[4,16,32,128]{3,2,1,0:T(8,128)}, u32[]{:S(2)}, u32[]{:S(2)}) async-start(f32[4,16,32,128]{3,2,1,0:T(8,128)} %copy.49), calls=%async_computation.1 | async-start | bytes 2097152 | tf_op jit(solution)/shard_map/all_to_all | solution.py:44
  48.0 0.0 copy-done
  48.0 12.4 %fusion = f32[16,576,128]{2,1,0:T(8,128)} fusion(f32[576,576]{1,0:T(8,128)} %subtract_maximum_fusion, f32[16]{0:T(128)S(1)} %get-tuple-element.5, pred[576,576]{1,0:T(8,128)(4,1)} %subtract_compare_fusion, bf16[576,2048]{1,0:T(8,128)(2,1)} %param.7, bf16[576,2048]{1,0:T(8,128)(2,1)} %param.6, bf16[576,2048]{1,0:T(8,128)(2,1)S(1)} %copy-done), kind=kOutput, calls=%fused_computation.1 | convolution fusion | flops 2744451072 | bytes 13455424 | tf_op jit(solution)/shard_map/hij,jhd->ihd/dot_general | solution.py:47
  60.5 3.1 %fusion.33 = f32[16,1,32,128]{3,1,2,0:T(1,128)} fusion(f32[4,16,1,1]{0,2,3,1:T(1,128)S(1)} %copy.54, f32[1,16,4,32,128]{4,1,3,2,0:T(8,128)S(1)} %bitcast.95), kind=kOutput, calls=%fused_computation.32 | convolution fusion | flops 3145728 | bytes 1310976 | tf_op jit(solution)/shard_map/mh,mhre->hre/dot_general | solution.py:43
  63.6 9.6 %all-to-all-done.1 = f32[4,16,32,128]{3,2,1,0:T(8,128)} async-done(((f32[4,16,32,128]{3,2,1,0:T(8,128)}), f32[4,16,32,128]{3,2,1,0:T(8,128)}, u32[]{:S(2)}, u32[]{:S(2)}) %all-to-all-start.1) | async-done | bytes 1048608 | tf_op jit(solution)/shard_map/all_to_all | solution.py:44
  73.2 1.3 %copy.50 = f32[4,16,32,128]{3,2,0,1:T(8,128)S(1)} copy(f32[4,16,32,128]{3,2,1,0:T(8,128)} %all-to-all-done.1) | data formatting | bytes 2097152 | tf_op jit(solution)/shard_map/all_to_all | solution.py:44
  74.5 0.0 copy-start.1
  74.5 8.2 %multiply_reduce_fusion = (f32[576]{0:T(1024)S(1)}, f32[576,16,128]{2,0,1:T(8,128)}) fusion(f32[16,128,128]{2,1,0:T(8,128)S(1)} %bitcast.96, f32[576,16]{0,1:T(8,128)S(1)} %get-tuple-element.2, f32[16,576,128]{2,1,0:T(8,128)} %fusion, bf16[576,2048]{1,0:T(8,128)(2,1)S(1)} %copy-done), kind=kOutput, calls=%fused_computation.8 | convolution fusion | flops 1817837056 | bytes 12884224 | tf_op jit(solution)/shard_map/ihd,hde->ihe/dot_general | solution.py:49
  82.7 0.2 dynamic-update-slice
  82.9 10.1 %all-reduce = f32[2304]{0:T(1024)S(1)} all-reduce(f32[2304]{0:T(1024)S(1)} %dynamic-update-slice), channel_id=2, replica_groups=mesh['groups'=2,'seq'=4,'head'=2,'sub'=2] {'head','sub'}, use_global_device_ids=true, to_apply=%add | all-reduce | flops 2304 | bytes 18432
  93.0 0.1 reshape.227
  93.2 0.0 copy-done.1
  93.2 4.2 %fusion.5 = bf16[576,2048]{1,0:T(8,128)(2,1)} fusion(f32[2048]{0:T(1024)S(1)} %copy-done.1, f32[576]{0:T(1024)S(1)} %add_rsqrt_fusion, f32[576,16,128]{2,0,1:T(8,128)} %get-tuple-element.7), kind=kLoop, calls=%fused_computation.6 | loop fusion | flops 3538944 | bytes 7088384 | tf_op jit(solution)/shard_map/convert_element_type | solution.py:54
  (8 shorter events, 0.0 us)
Async XLA Ops:
  0.6 47.4 %copy-start = (bf16[576,2048]{1,0:T(8,128)(2,1)S(1)}, bf16[576,2048]{1,0:T(8,128)(2,1)}, u32[]{:S(2)}) copy-start(bf16[576,2048]{1,0:T(8,128)(2,1)} %param.5) | copy-start | bytes 7077892
  6.3 8.1 %copy-start.2 = (u32[32]{0:T(128)S(1)}, u32[32]{0:T(128)}, u32[]{:S(2)}) copy-start(u32[32]{0:T(128)} %constant.8) | copy-start | bytes 388
  7.9 32.1 %all-to-all-start = ((f32[1,16,128,128]{3,1,0,2:T(8,128)}), f32[1,16,128,128]{3,1,0,2:T(8,128)S(1)}, u32[]{:S(2)}, u32[]{:S(2)}) async-start(f32[1,16,128,128]{3,1,0,2:T(8,128)} %copy.46), calls=%async_computation | async-start | bytes 2097152 | tf_op jit(solution)/shard_map/all_to_all | solution.py:31
  43.6 29.6 %all-to-all-start.1 = ((f32[4,16,32,128]{3,2,1,0:T(8,128)}), f32[4,16,32,128]{3,2,1,0:T(8,128)}, u32[]{:S(2)}, u32[]{:S(2)}) async-start(f32[4,16,32,128]{3,2,1,0:T(8,128)} %copy.49), calls=%async_computation.1 | async-start | bytes 2097152 | tf_op jit(solution)/shard_map/all_to_all | solution.py:44
  74.5 18.7 %copy-start.1 = (f32[2048]{0:T(1024)S(1)}, f32[2048]{0:T(1024)}, u32[]{:S(2)}) copy-start(f32[2048]{0:T(1024)} %param.9) | copy-start | bytes 24580
